TPU v7x, 256 devices: a whole 4x4x8 slice. The times are simulated.
256 devices in a mesh: ctx: 64 (over x, z, y_lo), tp: 4 (over y_hi, core).
Axes of the slice: x: 4, y: 4 (y_hi: 2, y_lo: 2; y = y_hi * 2 + y_lo), z: 8, core: 2. Of those that a mesh axis runs over, the one named last changes fastest.
Arguments:
- pre: float32 [3, 1024, 16384], P(None, 'tp', 'ctx'), may hold values from -6 to 6
- raw_filter: float32 [1024, 16384], P('tp', 'ctx'), may hold values from -6 to 6
- decay: float32 [1024], P('tp'), may hold values from 0 to 1, as said below
- taps: float32 [3, 3, 1024], P(None, None, 'tp'), may hold values from -3.5 to 3.5
- grad_out: float32 [1024, 16384], P(None, ('ctx', 'tp')), may hold values from -6 to 6
Outputs:
- grad_pre: float32 [3, 1024, 16384], P(None, 'tp', 'ctx')
- grad_filter: float32 [1024, 16384], P('tp', 'ctx')
- grad_taps: float32 [3, 3, 1024], P(None, None, 'tp')
Inputs may be any that keep to these rules, and one draw needn't show every extreme that they name: `decay`: rates per token between 0.3 / 16384 and 1 / 40.
All inputs are finite; a program needn't handle non-finite values.
Results may differ from a plain program's by a relative error of at most 0.00013.
Values sent between devices are 32-bit elements; how exact they have to be, the bound alone decides.
No kernel may reach another device: no remote copies, remote signals or barrier semaphores. Data moves between devices by JAX's collectives and lax.ppermute only.
A program may use at most 128 MiB of HBM per device.

v0:
```python
import math
import jax
import jax.numpy as jnp
from jax import lax
from jax.sharding import PartitionSpec as P


def passed_along(x, axis, by):
    devices = lax.axis_size(axis)
    pairs = [(i, i + by) for i in range(devices) if 0 <= i + by < devices]
    return lax.ppermute(x, axis, pairs)


def make_tables(outer_len, inner_len):
    total_len = outer_len * inner_len
    outer_index = jnp.arange(outer_len, dtype=jnp.int32)
    inner_index = jnp.arange(inner_len, dtype=jnp.int32)
    outer_angle = (outer_index[:, None] * outer_index[None, :] % outer_len).astype(jnp.float32) * (
        2.0 * math.pi / outer_len
    )
    inner_angle = (inner_index[:, None] * inner_index[None, :] % inner_len).astype(jnp.float32) * (
        2.0 * math.pi / inner_len
    )
    twist_angle = (outer_index[:, None] * inner_index[None, :] % total_len).astype(jnp.float32) * (
        2.0 * math.pi / total_len
    )
    return (
        jnp.cos(outer_angle),
        jnp.sin(outer_angle),
        jnp.cos(inner_angle),
        jnp.sin(inner_angle),
        jnp.cos(twist_angle),
        jnp.sin(twist_angle),
    )


def matmul_inner(blocks, table):
    return jnp.einsum("ncb,be->nce", blocks, table, precision=lax.Precision.HIGHEST)


def forward_spectrum(signal, tables, outer_len, inner_len):
    cos_outer, sin_outer, cos_inner, sin_inner, cos_twist, sin_twist = tables
    half_rows = outer_len // 2
    blocks = signal.reshape(signal.shape[0], half_rows, inner_len)
    real_a = jnp.einsum(
        "ca,nab->ncb", cos_outer[:, :half_rows], blocks, precision=lax.Precision.HIGHEST
    )
    imag_a = -jnp.einsum(
        "ca,nab->ncb", sin_outer[:, :half_rows], blocks, precision=lax.Precision.HIGHEST
    )
    real_b = real_a * cos_twist + imag_a * sin_twist
    imag_b = imag_a * cos_twist - real_a * sin_twist
    real_r = matmul_inner(real_b, cos_inner) + matmul_inner(imag_b, sin_inner)
    imag_r = matmul_inner(imag_b, cos_inner) - matmul_inner(real_b, sin_inner)
    return (real_r, imag_r)


def inverse_signal(real_r, imag_r, tables, outer_len, inner_len):
    cos_outer, sin_outer, cos_inner, sin_inner, cos_twist, sin_twist = tables
    half_rows = outer_len // 2
    real_s = matmul_inner(real_r, cos_inner) - matmul_inner(imag_r, sin_inner)
    imag_s = matmul_inner(imag_r, cos_inner) + matmul_inner(real_r, sin_inner)
    real_t = real_s * cos_twist - imag_s * sin_twist
    imag_t = imag_s * cos_twist + real_s * sin_twist
    signal = jnp.einsum(
        "ac,ncb->nab", cos_outer[:half_rows], real_t, precision=lax.Precision.HIGHEST
    )
    signal = signal - jnp.einsum(
        "ac,ncb->nab", sin_outer[:half_rows], imag_t, precision=lax.Precision.HIGHEST
    )
    signal = signal * (1.0 / (outer_len * inner_len))
    return signal.reshape(signal.shape[0], half_rows * inner_len)


def long_terms(product, kernel, grad_gate, outer_len, inner_len):
    tables = make_tables(outer_len, inner_len)
    kernel_re, kernel_im = forward_spectrum(kernel, tables, outer_len, inner_len)
    product_re, product_im = forward_spectrum(product, tables, outer_len, inner_len)
    gate_re, gate_im = forward_spectrum(grad_gate, tables, outer_len, inner_len)
    mixed_long = inverse_signal(
        kernel_re * product_re - kernel_im * product_im,
        kernel_re * product_im + kernel_im * product_re,
        tables,
        outer_len,
        inner_len,
    )
    grad_product = inverse_signal(
        kernel_re * gate_re + kernel_im * gate_im,
        kernel_re * gate_im - kernel_im * gate_re,
        tables,
        outer_len,
        inner_len,
    )
    grad_kernel = inverse_signal(
        product_re * gate_re + product_im * gate_im,
        product_re * gate_im - product_im * gate_re,
        tables,
        outer_len,
        inner_len,
    )
    return (mixed_long, grad_product, grad_kernel)


def local(pre, raw_filter, decay, taps, grad_out):
    tap_count = taps.shape[1]
    reach = tap_count - 1
    tok_dev = pre.shape[2]
    ctx_count = lax.axis_size("ctx")
    seq_len = tok_dev * ctx_count
    outer_len = 4 * ctx_count
    inner_len = tok_dev // 2
    before = passed_along(pre[:, :, tok_dev - reach :], "ctx", 1)
    extended = jnp.concatenate([before, pre], axis=2)
    featured = taps[:, 0, :, None] * extended[:, :, reach : reach + tok_dev]
    for j in range(1, tap_count):
        featured = featured + taps[:, j, :, None] * extended[:, :, reach - j : reach - j + tok_dev]
    query_post, key_post, value_post = (featured[0], featured[1], featured[2])
    offset = lax.axis_index("ctx") * tok_dev
    positions = (offset + jnp.arange(tok_dev, dtype=jnp.int32)).astype(jnp.float32)
    envelope = jnp.exp(-decay[:, None] * positions[None, :]) * (1.0 / math.sqrt(seq_len))
    kernel = raw_filter * envelope
    tp_count = lax.axis_size("tp")
    sliver_width = grad_out.shape[0] // (tp_count * ctx_count)
    arranged = grad_out.reshape(tp_count, ctx_count, sliver_width, grad_out.shape[1])
    grad_sliver = lax.all_to_all(
        lax.all_to_all(arranged, "tp", split_axis=0, concat_axis=3, tiled=True),
        "ctx",
        split_axis=1,
        concat_axis=3,
        tiled=True,
    ).reshape(sliver_width, seq_len)
    packed = jnp.stack([query_post, key_post, value_post, kernel])
    slivers = lax.all_to_all(packed, "ctx", split_axis=1, concat_axis=2, tiled=True)
    product = slivers[1] * slivers[2]
    grad_gate = grad_sliver * slivers[0]
    mixed_long, grad_product, grad_kernel = long_terms(
        product, slivers[3], grad_gate, outer_len, inner_len
    )
    results = jnp.stack(
        [
            grad_sliver * mixed_long,
            grad_product * slivers[2],
            grad_product * slivers[1],
            grad_kernel,
        ]
    )
    returned = lax.all_to_all(results, "ctx", split_axis=2, concat_axis=1, tiled=True)
    grad_featured = returned[:3]
    kernel_grad_tok = returned[3]
    after = passed_along(grad_featured[:, :, :reach], "ctx", -1)
    grad_extended = jnp.concatenate([grad_featured, after], axis=2)
    grad_pre = taps[:, 0, :, None] * grad_extended[:, :, 0:tok_dev]
    for j in range(1, tap_count):
        grad_pre = grad_pre + taps[:, j, :, None] * grad_extended[:, :, j : j + tok_dev]
    tap_terms = [
        jnp.sum(grad_featured * extended[:, :, reach - j : reach - j + tok_dev], axis=2)
        for j in range(tap_count)
    ]
    local_taps = jnp.stack(tap_terms, axis=1)
    grad_taps = lax.psum(local_taps, "ctx") * (1.0 / math.sqrt(seq_len))
    grad_filter = kernel_grad_tok * envelope
    return (grad_pre, grad_filter, grad_taps)


def solution(mesh):
    in_specs = (
        P(None, "tp", "ctx"),
        P("tp", "ctx"),
        P("tp"),
        P(None, None, "tp"),
        P(None, ("ctx", "tp")),
    )
    out_specs = (P(None, "tp", "ctx"), P("tp", "ctx"), P(None, None, "tp"))
    return jax.shard_map(local, mesh=mesh, in_specs=in_specs, out_specs=out_specs, check_vma=False)
```

profile of v0, /device:TPU:16, one launch (start us, length us, event | category | flops | bytes accessed | tf_op | source)
XLA Modules:
  0.0 629.1 jit_solution(6635581628537031192)
XLA Ops:
  2.0 3.2 collective-permute-start
  7.6 4.8 all-to-all-start
  12.5 4.2 all-to-all-done
  20.4 12.6 %all-to-all-start.1 = ((f32[1,64,4,256]{3,2,0,1:T(4,128)}), f32[1,64,4,256]{3,2,0,1:T(4,128)S(1)}, u32[]{:S(2)}, u32[]{:S(2)}) async-start(f32[1,64,4,256]{3,2,0,1:T(4,128)} %reshape.147), calls=%async_computation.1 | async-start | bytes 524288 | tf_op jit(solution)/shard_map/all_to_all | solution.py:125
  34.6 2.5 multiply_add_fusion
  38.6 6.6 %all-to-all-done.1 = f32[1,64,4,256]{3,2,0,1:T(4,128)S(1)} async-done(((f32[1,64,4,256]{3,2,0,1:T(4,128)}), f32[1,64,4,256]{3,2,0,1:T(4,128)S(1)}, u32[]{:S(2)}, u32[]{:S(2)}) %all-to-all-start.1) | async-done | bytes 262176 | tf_op jit(solution)/shard_map/all_to_all | solution.py:125
  45.2 6.2 all-to-all-start.2
  54.0 25.6 %all-to-all-done.2 = f32[4,256,256]{2,0,1:T(4,128)S(1)} async-done(((f32[4,256,256]{2,0,1:T(4,128)}), f32[4,256,256]{2,0,1:T(4,128)S(1)}, u32[]{:S(2)}, u32[]{:S(2)}) %all-to-all-start.2) | async-done | bytes 1048608 | tf_op jit(solution)/shard_map/all_to_all | solution.py:133
  87.6 2.0 fusion.96
  89.6 2.0 fusion.100
  93.6 2.2 fusion.90
  95.8 2.0 fusion.98
  97.8 2.0 fusion.102
  103.4 2.3 convolution_subtract_fusion.4
  130.7 20.5 %copy.280 = f32[4,4,16384]{1,0,2:T(4,128)} copy(f32[4,4,16384]{2,1,0:T(4,128)S(1)} %pad_maximum_fusion.3) | data formatting | bytes 2097152 | tf_op jit(solution)/shard_map/stack | solution.py:139
  151.1 40.5 %reshape.150 = f32[64,1,4096]{2,1,0:T(1,128)S(1)} reshape(f32[16384,4,4]{2,1,0:T(4,128)} %bitcast.144) | data formatting | bytes 2097152
  191.7 34.2 %all_to_all.63 = f32[64,1,4096]{2,1,0:T(1,128)S(1)} all-to-all(f32[64,1,4096]{2,1,0:T(1,128)S(1)} %reshape.150), channel_id=1, replica_groups=mesh['ctx'=64,'tp'=4] {'ctx'}, dimensions={0} | all-to-all | bytes 2097152 | tf_op jit(solution)/shard_map/all_to_all | solution.py:147
  225.8 3.3 reduce.1
  229.1 45.5 %reshape.151 = f32[16384,4,4]{2,1,0:T(4,128)} reshape(f32[64,4096]{1,0:T(8,128)S(1)} %reduce.1) | data formatting | bytes 2097152
  274.6 24.2 %copy.281 = f32[4,4,64,256]{3,1,2,0:T(4,128)S(1)} copy(f32[4,4,64,256]{1,0,3,2:T(4,128)} %bitcast.145) | data formatting | bytes 2097152 | tf_op jit(solution)/shard_map/all_to_all | solution.py:147
  305.7 2.4 collective-permute-done.1
  309.8 8.9 %multiply_reduce_fusion.1 = (f32[3,256]{0,1:T(8,128)}, f32[3,256]{0,1:T(8,128)}, f32[3,256]{0,1:T(8,128)}, f32[3,256,256]{2,0,1:T(4,128)}) fusion(f32[3,256,256]{2,0,1:T(4,128)S(1)} %bitcast.147, f32[3,256,256]{2,0,1:T(4,128)S(1)} %copy-done.1, f32[3,256,2]{2,0,1:T(4,128)S(1)} %copy-done.5, f32[3,256,256]{2,1,0:T(8,128)S(1)} %copy-done.3, ...), kind=kLoop, calls=%fused_computation.46 | loop fusion | flops 2946816 | bytes 3176448 | tf_op jit(solution)/shard_map/reduce_sum | solution.py:156
  321.6 304.4 %psum.7 = f32[3,3,256]{2,0,1:T(4,128)S(1)} all-reduce(f32[3,3,256]{2,0,1:T(4,128)S(1)} %pad_maximum_fusion.4), channel_id=1, replica_groups=mesh['ctx'=64,'tp'=4] {'ctx'}, use_global_device_ids=true, to_apply=%region_3.4 | all-reduce | flops 2304 | bytes 18432 | tf_op jit(solution)/shard_map/psum | solution.py:160
  626.6 2.3 copy.289
  (149 shorter events, 63.3 us)
Async XLA Ops:
  0.6 11.8 %copy-start.30 = (f32[256]{0:T(256)S(1)}, f32[256]{0:T(256)}, u32[]{:S(2)}) copy-start(f32[256]{0:T(256)} %param.7) | copy-start | bytes 3076
  0.6 11.8 %copy-start.28 = (f32[256,256]{1,0:T(8,128)S(1)}, f32[256,256]{1,0:T(8,128)}, u32[]{:S(2)}) copy-start(f32[256,256]{1,0:T(8,128)} %param.6) | copy-start | bytes 786436
  2.0 32.3 %collective-permute-start = (f32[3,256,2]{1,0,2:T(4,128)S(1)}, f32[3,256,2]{1,0,2:T(4,128)S(1)}, u32[]{:S(2)}, u32[]{:S(2)}) collective-permute-start(f32[3,256,2]{1,0,2:T(4,128)S(1)} %copy.326), channel_id=1, source_target_pairs={{0,4},{4,8},{8,12},{12,16},{16,20},{20,24},{24,28},{28,32},{32,36}... | collective-permute-start | bytes 18440 | tf_op jit(solution)/shard_map/ppermute | solution.py:11
  7.6 9.2 %all-to-all-start = ((f32[4,1,16384]{2,1,0:T(1,128)}), f32[4,1,16384]{2,1,0:T(1,128)S(1)}, u32[]{:S(2)}, u32[]{:S(2)}) async-start(f32[4,1,16384]{2,1,0:T(1,128)} %reshape.148), calls=%async_computation | async-start | bytes 524288 | tf_op jit(solution)/shard_map/all_to_all | solution.py:126
  18.6 14.4 %copy-start.29 = (f32[3,3,256]{2,1,0:T(4,128)S(1)}, f32[3,3,256]{2,1,0:T(4,128)}, u32[]{:S(2)}) copy-start(f32[3,3,256]{2,1,0:T(4,128)} %param.8) | copy-start | bytes 27652
  18.7 14.4 %copy-start.2 = (f32[3,256,256]{2,1,0:T(8,128)S(1)}, f32[3,256,256]{2,1,0:T(8,128)}, u32[]{:S(2)}) copy-start(f32[3,256,256]{2,1,0:T(8,128)} %param.5) | copy-start | bytes 2359300
  20.4 24.7 %all-to-all-start.1 = ((f32[1,64,4,256]{3,2,0,1:T(4,128)}), f32[1,64,4,256]{3,2,0,1:T(4,128)S(1)}, u32[]{:S(2)}, u32[]{:S(2)}) async-start(f32[1,64,4,256]{3,2,0,1:T(4,128)} %reshape.147), calls=%async_computation.1 | async-start | bytes 524288 | tf_op jit(solution)/shard_map/all_to_all | solution.py:125
  33.6 3.5 copy-start
  33.9 3.2 copy-start.22
  34.1 3.1 copy-start.23
  34.6 4.0 copy-start.4
  45.2 8.7 %copy-start.14 = (f32[1,64,4,256]{3,2,0,1:T(4,128)}, f32[1,64,4,256]{3,2,0,1:T(4,128)S(1)}, u32[]{:S(2)}) copy-start(f32[1,64,4,256]{3,2,0,1:T(4,128)S(1)} %all-to-all-done.1) | copy-start | bytes 786436
  45.2 34.4 %all-to-all-start.2 = ((f32[4,256,256]{2,0,1:T(4,128)}), f32[4,256,256]{2,0,1:T(4,128)S(1)}, u32[]{:S(2)}, u32[]{:S(2)}) async-start(f32[4,256,256]{2,0,1:T(4,128)} %pad_maximum_fusion.2), calls=%async_computation.2 | async-start | bytes 2097152 | tf_op jit(solution)/shard_map/all_to_all | solution.py:133
  52.3 30.7 %copy-start.6 = (f32[256,256]{1,0:T(8,128)}, f32[256,256]{1,0:T(8,128)S(1)}, u32[]{:S(2)}) copy-start(f32[256,256]{1,0:T(8,128)S(1)} %fusion.61) | copy-start | bytes 786436
  53.3 31.3 %copy-start.10 = (f32[256,256]{1,0:T(8,128)}, f32[256,256]{1,0:T(8,128)S(1)}, u32[]{:S(2)}) copy-start(f32[256,256]{1,0:T(8,128)S(1)} %fusion.60) | copy-start | bytes 786436
  82.4 2.2 copy-start.27
  103.4 2.3 copy-start.20
  114.2 1.8 copy-start.7
  121.5 1.8 copy-start.8
  126.5 1.8 copy-start.9
  300.3 9.5 %copy-start.1 = (f32[3,256,256]{2,0,1:T(4,128)S(1)}, f32[3,256,256]{2,0,1:T(4,128)}, u32[]{:S(2)}) copy-start(f32[3,256,256]{2,0,1:T(4,128)} %copy-done) | copy-start | bytes 2359300
  300.3 9.5 %copy-start.3 = (f32[3,256,256]{2,1,0:T(8,128)S(1)}, f32[3,256,256]{2,1,0:T(8,128)}, u32[]{:S(2)}) copy-start(f32[3,256,256]{2,1,0:T(8,128)} %param.5) | copy-start | bytes 2359300
  300.3 9.5 %copy-start.5 = (f32[3,256,2]{2,0,1:T(4,128)S(1)}, f32[3,256,2]{2,0,1:T(4,128)}, u32[]{:S(2)}) copy-start(f32[3,256,2]{2,0,1:T(4,128)} %copy-done.4) | copy-start | bytes 18436
  302.4 5.7 collective-permute-start.1
  (12 other events, 14.1 us)
where the time goes:
time: 636 us; the launch traced here: 629 us
  blocking collectives  339 us (53%)
  local copies, waits for them, and re-layouts  157 us (25%)
  matrix products  41.7 us (7%)
  waiting for transfers between devices  38.8 us (6%)
  starting transfers between devices  28.2 us (4%)
  other arithmetic  23.2 us (4%)
    psum x1, blocking collectives, local(): grad_taps = lax.psum(local_taps, 'ctx') * (1.0 / math.sqrt(seq_len))  304 us
    unnamed x71, local copies, waits for them, and re-layouts  93.3 us
    all_to_all x1, blocking collectives, local(): lax.all_to_all(results, 'ctx', split_axis=2, concat_axis=1, tiled=True)  34.2 us
    dot_general x24, matrix products, matmul_inner(): jnp.einsum('ncb,be->nce', blocks, table, precision=lax.Precision.HIGHEST)  31.6 us
    all_to_all x1, waiting for transfers between devices, local(): lax.all_to_all(packed, 'ctx', split_axis=1, concat_axis=2, tiled=True)  25.6 us
    all_to_all x1, local copies, waits for them, and re-layouts, local(): lax.all_to_all(results, 'ctx', split_axis=2, concat_axis=1, tiled=True)  24.2 us
    another operation x2, local copies, waits for them, and re-layouts, local(): jnp.stack([grad_sliver * mixed_long, grad_product * slivers[2], grad_prod...  20.6 us
  transfers between devices with their start and end apart: 5, of which 4 were waited for; matrix products, arithmetic and copies ran while one was open for 3% of the time, Pallas kernels for 0%

commit v1 on v0

--- a/solution.py
+++ b/solution.py
@@ -157,7 +157,7 @@
         for j in range(tap_count)
     ]
     local_taps = jnp.stack(tap_terms, axis=1)
-    grad_taps = lax.psum(local_taps, "ctx") * (1.0 / math.sqrt(seq_len))
+    grad_taps = jnp.sum(lax.all_gather(local_taps, "ctx"), axis=0) * (1.0 / math.sqrt(seq_len))
     grad_filter = kernel_grad_tok * envelope
     return (grad_pre, grad_filter, grad_taps)
 

time: 636 us -> 488 us (0.77)
  blocking collectives: 339 us -> 190 us
    psum x1 -> x0, blocking collectives: 304 us -> none  [local(): grad_taps = lax.psum(local_taps, 'ctx') * (1.0 / math.sqrt(seq_len))]
    all_gather x0 -> x1, blocking collectives: none -> 156 us  [local(): lax.all_gather(local_taps, 'ctx')]
where the time goes in v1:
time: 488 us; the launch traced here: 481 us
  blocking collectives  190 us (39%)
  local copies, waits for them, and re-layouts  156 us (32%)
  matrix products  42.6 us (9%)
  waiting for transfers between devices  38.8 us (8%)
  starting transfers between devices  28.2 us (6%)
  other arithmetic  23.3 us (5%)
    all_gather x1, blocking collectives, local(): lax.all_gather(local_taps, 'ctx')  156 us
    unnamed x71, local copies, waits for them, and re-layouts  91.4 us
    all_to_all x1, blocking collectives, local(): lax.all_to_all(results, 'ctx', split_axis=2, concat_axis=1, tiled=True)  34.2 us
    dot_general x24, matrix products, matmul_inner(): jnp.einsum('ncb,be->nce', blocks, table, precision=lax.Precision.HIGHEST)  31.6 us
    all_to_all x1, waiting for transfers between devices, local(): lax.all_to_all(packed, 'ctx', split_axis=1, concat_axis=2, tiled=True)  25.6 us
    all_to_all x1, local copies, waits for them, and re-layouts, local(): lax.all_to_all(results, 'ctx', split_axis=2, concat_axis=1, tiled=True)  24.2 us
    another operation x2, local copies, waits for them, and re-layouts, local(): jnp.stack([grad_sliver * mixed_long, grad_product * slivers[2], grad_prod...  20.6 us
    all_to_all x1, starting transfers between devices, local(): lax.all_to_all(lax.all_to_all(arranged, 'tp', split_axis=0, concat_axis=3...  12.6 us
  transfers between devices with their start and end apart: 5, of which 4 were waited for; matrix products, arithmetic and copies ran while one was open for 3% of the time, Pallas kernels for 0%

profile of v1, /device:TPU:16, one launch (start us, length us, event | category | flops | bytes accessed | tf_op | source)
XLA Modules:
  0.0 480.6 jit_solution(14643431343657749393)
XLA Ops:
  2.0 3.2 collective-permute-start
  7.6 4.8 all-to-all-start
  12.5 4.2 all-to-all-done
  20.4 12.6 %all-to-all-start.1 = ((f32[1,64,4,256]{3,2,0,1:T(4,128)}), f32[1,64,4,256]{3,2,0,1:T(4,128)S(1)}, u32[]{:S(2)}, u32[]{:S(2)}) async-start(f32[1,64,4,256]{3,2,0,1:T(4,128)} %reshape.148), calls=%async_computation.1 | async-start | bytes 524288 | tf_op jit(solution)/shard_map/all_to_all | solution.py:125
  34.6 2.5 multiply_add_fusion
  38.6 6.6 %all-to-all-done.1 = f32[1,64,4,256]{3,2,0,1:T(4,128)S(1)} async-done(((f32[1,64,4,256]{3,2,0,1:T(4,128)}), f32[1,64,4,256]{3,2,0,1:T(4,128)S(1)}, u32[]{:S(2)}, u32[]{:S(2)}) %all-to-all-start.1) | async-done | bytes 262176 | tf_op jit(solution)/shard_map/all_to_all | solution.py:125
  45.2 6.2 %all-to-all-start.2 = ((f32[4,256,256]{2,0,1:T(4,128)}), f32[4,256,256]{2,0,1:T(4,128)S(1)}, u32[]{:S(2)}, u32[]{:S(2)}) async-start(f32[4,256,256]{2,0,1:T(4,128)} %pad_maximum_fusion.2), calls=%async_computation.2 | async-start | bytes 2097152 | tf_op jit(solution)/shard_map/all_to_all | solution.py:133
  54.0 25.6 %all-to-all-done.2 = f32[4,256,256]{2,0,1:T(4,128)S(1)} async-done(((f32[4,256,256]{2,0,1:T(4,128)}), f32[4,256,256]{2,0,1:T(4,128)S(1)}, u32[]{:S(2)}, u32[]{:S(2)}) %all-to-all-start.2) | async-done | bytes 1048608 | tf_op jit(solution)/shard_map/all_to_all | solution.py:133
  88.5 2.0 fusion.96
  90.5 2.0 fusion.100
  92.5 2.0 fusion.88
  94.5 2.2 fusion.90
  96.8 2.0 fusion.98
  98.8 2.0 fusion.102
  104.3 2.3 convolution_subtract_fusion.4
  131.6 20.5 %copy.343 = f32[4,4,16384]{1,0,2:T(4,128)} copy(f32[4,4,16384]{2,1,0:T(4,128)S(1)} %pad_maximum_fusion.3) | data formatting | bytes 2097152 | tf_op jit(solution)/shard_map/stack | solution.py:139
  152.1 40.5 %reshape.151 = f32[64,1,4096]{2,1,0:T(1,128)S(1)} reshape(f32[16384,4,4]{2,1,0:T(4,128)} %bitcast.145) | data formatting | bytes 2097152
  192.6 34.2 %all_to_all.63 = f32[64,1,4096]{2,1,0:T(1,128)S(1)} all-to-all(f32[64,1,4096]{2,1,0:T(1,128)S(1)} %reshape.151), channel_id=1, replica_groups=mesh['ctx'=64,'tp'=4] {'ctx'}, dimensions={0} | all-to-all | bytes 2097152 | tf_op jit(solution)/shard_map/all_to_all | solution.py:147
  226.7 3.3 reduce.1
  230.0 45.5 %reshape.152 = f32[16384,4,4]{2,1,0:T(4,128)} reshape(f32[64,4096]{1,0:T(8,128)S(1)} %reduce.1) | data formatting | bytes 2097152
  275.5 24.2 %copy.344 = f32[4,4,64,256]{3,1,2,0:T(4,128)S(1)} copy(f32[4,4,64,256]{1,0,3,2:T(4,128)} %bitcast.146) | data formatting | bytes 2097152 | tf_op jit(solution)/shard_map/all_to_all | solution.py:147
  306.6 2.4 collective-permute-done.1
  310.7 8.9 %multiply_reduce_fusion.1 = (f32[3,256]{0,1:T(8,128)}, f32[3,256]{0,1:T(8,128)}, f32[3,256]{0,1:T(8,128)}, f32[3,256,256]{2,0,1:T(4,128)}) fusion(f32[3,256,256]{2,0,1:T(4,128)S(1)} %bitcast.148, f32[3,256,256]{2,0,1:T(4,128)S(1)} %copy-done.1, f32[3,256,2]{2,0,1:T(4,128)S(1)} %copy-done.5, f32[3,256,256]{2,1,0:T(8,128)S(1)} %copy-done.3, ...), kind=kLoop, calls=%fused_computation.46 | loop fusion | flops 2946816 | bytes 3176448 | tf_op jit(solution)/shard_map/reduce_sum | solution.py:156
  322.6 155.9 %all-gather = f32[192,3,256]{2,1,0:T(4,128)S(1)} all-gather(f32[3,3,256]{2,1,0:T(4,128)S(1)} %pad_maximum_fusion.4), channel_id=2, replica_groups=mesh['ctx'=64,'tp'=4] {'ctx'}, dimensions={0}, use_global_device_ids=true | all-gather | bytes 599040 | tf_op jit(solution)/shard_map/all_gather | solution.py:160
  (150 shorter events, 63.5 us)
Async XLA Ops:
  0.6 11.8 %copy-start.30 = (f32[256]{0:T(256)S(1)}, f32[256]{0:T(256)}, u32[]{:S(2)}) copy-start(f32[256]{0:T(256)} %param.7) | copy-start | bytes 3076
  0.6 11.8 %copy-start.28 = (f32[256,256]{1,0:T(8,128)S(1)}, f32[256,256]{1,0:T(8,128)}, u32[]{:S(2)}) copy-start(f32[256,256]{1,0:T(8,128)} %param.6) | copy-start | bytes 786436
  2.0 32.3 %collective-permute-start = (f32[3,256,2]{1,0,2:T(4,128)S(1)}, f32[3,256,2]{1,0,2:T(4,128)S(1)}, u32[]{:S(2)}, u32[]{:S(2)}) collective-permute-start(f32[3,256,2]{1,0,2:T(4,128)S(1)} %copy.392), channel_id=1, source_target_pairs={{0,4},{4,8},{8,12},{12,16},{16,20},{20,24},{24,28},{28,32},{32,36}... | collective-permute-start | bytes 18440 | tf_op jit(solution)/shard_map/ppermute | solution.py:11
  7.6 9.2 %all-to-all-start = ((f32[4,1,16384]{2,1,0:T(1,128)}), f32[4,1,16384]{2,1,0:T(1,128)S(1)}, u32[]{:S(2)}, u32[]{:S(2)}) async-start(f32[4,1,16384]{2,1,0:T(1,128)} %reshape.149), calls=%async_computation | async-start | bytes 524288 | tf_op jit(solution)/shard_map/all_to_all | solution.py:126
  18.6 14.4 %copy-start.29 = (f32[3,3,256]{2,1,0:T(4,128)S(1)}, f32[3,3,256]{2,1,0:T(4,128)}, u32[]{:S(2)}) copy-start(f32[3,3,256]{2,1,0:T(4,128)} %param.8) | copy-start | bytes 27652
  18.7 14.4 %copy-start.2 = (f32[3,256,256]{2,1,0:T(8,128)S(1)}, f32[3,256,256]{2,1,0:T(8,128)}, u32[]{:S(2)}) copy-start(f32[3,256,256]{2,1,0:T(8,128)} %param.5) | copy-start | bytes 2359300
  20.4 24.7 %all-to-all-start.1 = ((f32[1,64,4,256]{3,2,0,1:T(4,128)}), f32[1,64,4,256]{3,2,0,1:T(4,128)S(1)}, u32[]{:S(2)}, u32[]{:S(2)}) async-start(f32[1,64,4,256]{3,2,0,1:T(4,128)} %reshape.148), calls=%async_computation.1 | async-start | bytes 524288 | tf_op jit(solution)/shard_map/all_to_all | solution.py:125
  33.6 3.5 copy-start
  33.9 3.2 copy-start.22
  34.1 3.1 copy-start.23
  34.6 4.0 copy-start.4
  45.2 8.7 %copy-start.14 = (f32[1,64,4,256]{3,2,0,1:T(4,128)}, f32[1,64,4,256]{3,2,0,1:T(4,128)S(1)}, u32[]{:S(2)}) copy-start(f32[1,64,4,256]{3,2,0,1:T(4,128)S(1)} %all-to-all-done.1) | copy-start | bytes 786436
  45.2 34.4 %all-to-all-start.2 = ((f32[4,256,256]{2,0,1:T(4,128)}), f32[4,256,256]{2,0,1:T(4,128)S(1)}, u32[]{:S(2)}, u32[]{:S(2)}) async-start(f32[4,256,256]{2,0,1:T(4,128)} %pad_maximum_fusion.2), calls=%async_computation.2 | async-start | bytes 2097152 | tf_op jit(solution)/shard_map/all_to_all | solution.py:133
  52.3 30.7 %copy-start.7 = (f32[256,256]{1,0:T(8,128)}, f32[256,256]{1,0:T(8,128)S(1)}, u32[]{:S(2)}) copy-start(f32[256,256]{1,0:T(8,128)S(1)} %fusion.61) | copy-start | bytes 786436
  53.3 32.0 %copy-start.11 = (f32[256,256]{1,0:T(8,128)}, f32[256,256]{1,0:T(8,128)S(1)}, u32[]{:S(2)}) copy-start(f32[256,256]{1,0:T(8,128)S(1)} %fusion.60) | copy-start | bytes 786436
  82.4 2.2 copy-start.27
  104.3 2.3 copy-start.20
  115.1 1.8 copy-start.8
  127.5 1.8 copy-start.10
  301.2 9.5 %copy-start.1 = (f32[3,256,256]{2,0,1:T(4,128)S(1)}, f32[3,256,256]{2,0,1:T(4,128)}, u32[]{:S(2)}) copy-start(f32[3,256,256]{2,0,1:T(4,128)} %copy-done) | copy-start | bytes 2359300
  301.2 9.5 %copy-start.3 = (f32[3,256,256]{2,1,0:T(8,128)S(1)}, f32[3,256,256]{2,1,0:T(8,128)}, u32[]{:S(2)}) copy-start(f32[3,256,256]{2,1,0:T(8,128)} %param.5) | copy-start | bytes 2359300
  301.2 9.5 %copy-start.5 = (f32[3,256,2]{2,0,1:T(4,128)S(1)}, f32[3,256,2]{2,0,1:T(4,128)}, u32[]{:S(2)}) copy-start(f32[3,256,2]{2,0,1:T(4,128)} %copy-done.4) | copy-start | bytes 18436
  303.3 5.7 %collective-permute-start.1 = (f32[3,256,2]{1,0,2:T(4,128)S(1)}, f32[3,256,2]{1,0,2:T(4,128)}, u32[]{:S(2)}, u32[]{:S(2)}) collective-permute-start(f32[3,256,2]{1,0,2:T(4,128)S(1)} %copy.346), channel_id=1, source_target_pairs={{4,0},{8,4},{12,8},{16,12},{20,16},{24,20},{28,24},{32,28},{36,32}... | collective-permute-start | bytes 18440 | tf_op jit(solution)/shard_map/ppermute | solution.py:11
  319.6 159.8 %copy-start.6 = (f32[3,256,256]{2,0,1:T(4,128)S(1)}, f32[3,256,256]{2,0,1:T(4,128)}, u32[]{:S(2)}) copy-start(f32[3,256,256]{2,0,1:T(4,128)} %get-tuple-element.27) | copy-start | bytes 2359300
  (12 other events, 15.2 us)
